TPU v7x, 512 devices: a whole 4x8x8 slice. The times are simulated.
512 devices in a mesh: expert: 16 (over x, y_hi), tensor: 32 (over z, y_lo, core).
Axes of the slice: x: 4, y: 8 (y_hi: 4, y_lo: 2; y = y_hi * 2 + y_lo), z: 8, core: 2. Of those that a mesh axis runs over, the one named last changes fastest.
Arguments:
- tokens: bfloat16 [2048, 6144], P('expert'), may hold values from -6 to 6
- routes: int32 [2048, 4], P('expert'), may hold values from 0 to 15, all different within a row; in each aligned block of 128 rows (0 to 127, 128 to 255, ...) at most 40 rows name the same one
- gates: float32 [2048, 4], P('expert'), may hold values from 0.05 to 1
- gate_proj: bfloat16 [16, 2688, 6144], P('expert', 'tensor'), may hold values from -0.078125 to 0.078125
- up_proj: bfloat16 [16, 2688, 6144], P('expert', 'tensor'), may hold values from -0.078125 to 0.078125
- down_proj: bfloat16 [16, 6144, 2688], P('expert', 'tensor'), may hold values from -0.0625 to 0.0625
Outputs:
- combined: bfloat16 [2048, 6144], P('expert', 'tensor')
Inputs may be any that keep to these rules, and one draw needn't show every extreme that they name: `routes`: the ids of one row are distinct. In each aligned block of 128 rows no id is named by more than 40 rows, a bound that some block reaches.
All inputs are finite; a program needn't handle non-finite values.
Results may differ from a plain program's by a relative error of at most 0.0057.
Values may be sent and summed in bfloat16 or wider, within the bound.
No kernel may reach another device: no remote copies, remote signals or barrier semaphores. Data moves between devices by JAX's collectives and lax.ppermute only.
A program may use at most 64 MiB of HBM per device.

v0:
```python
import jax
import jax.numpy as jnp
from jax import lax
from jax.sharding import PartitionSpec as P

WIN = 4
CAP = 40


def slot_tables(route_block, gate_block):
    row_count = route_block.shape[0]
    experts = jnp.arange(WIN, dtype=jnp.int32)
    hits = route_block[None, :, :] == experts[:, None, None]
    chosen = jnp.any(hits, axis=2)
    position = jnp.cumsum(chosen.astype(jnp.int32), axis=1) - 1
    slots = jnp.arange(CAP, dtype=jnp.int32)
    match = chosen[:, None, :] & (position[:, None, :] == slots[None, :, None])
    row_ids = jnp.arange(row_count, dtype=jnp.int32)
    row_index = jnp.sum(jnp.where(match, row_ids[None, None, :], 0), axis=2)
    filled = jnp.any(match, axis=2)
    weight = jnp.sum(
        jnp.where(hits, gate_block[None, :, :], jnp.zeros((), gate_block.dtype)), axis=2
    )
    return (position, row_index, filled, weight)


def contract_last(left, right):
    return lax.dot_general(
        left, right, (((1,), (1,)), ((), ())), preferred_element_type=jnp.float32
    )


def body(tokens, routes, gates, gate_proj, up_proj, down_proj):
    groups = lax.axis_size("expert")
    split = groups // WIN
    width = tokens.shape[1]
    w_gate = gate_proj[0]
    w_up = up_proj[0]
    w_down = down_proj[0]
    position, row_index, filled, weight = slot_tables(routes, gates)
    picked = jnp.take(tokens, row_index, axis=0)
    picked = jnp.where(filled[:, :, None], picked, jnp.zeros((), tokens.dtype))
    outgoing = jnp.repeat(picked, split, axis=0)
    slot_rows = groups * CAP
    arrived = lax.all_to_all(outgoing, "expert", split_axis=0, concat_axis=0, tiled=True)
    flat_rows = arrived.reshape(slot_rows, width)
    gate_act = contract_last(flat_rows, w_gate)
    up_act = contract_last(flat_rows, w_up)
    hidden = (jax.nn.silu(gate_act) * up_act).astype(jnp.bfloat16)
    partial_value = contract_last(lax.all_gather(hidden, "tensor", axis=1, tiled=True), w_down)
    partial_value = partial_value.astype(jnp.bfloat16).reshape(groups, CAP, w_down.shape[0])
    returned = lax.all_to_all(partial_value, "expert", split_axis=0, concat_axis=0, tiled=True)
    expert_out = returned.astype(jnp.float32).reshape(WIN, split, CAP, w_down.shape[0]).sum(axis=1)
    flat_sum = expert_out.reshape(WIN * CAP, w_down.shape[0])
    offsets = jnp.arange(WIN, dtype=jnp.int32)[:, None] * CAP
    index = offsets + jnp.clip(position, 0, CAP - 1)
    values = jnp.take(flat_sum, index, axis=0)
    return jnp.sum(values * weight[:, :, None], axis=0).astype(jnp.bfloat16)


def solution(mesh):
    in_specs = (
        P("expert", None),
        P("expert", None),
        P("expert", None),
        P("expert", "tensor", None),
        P("expert", "tensor", None),
        P("expert", "tensor", None),
    )
    out_specs = P("expert", "tensor")
    return jax.shard_map(body, mesh=mesh, in_specs=in_specs, out_specs=out_specs, check_vma=False)
```

profile of v0, /device:TPU:8, one launch (start us, length us, event | category | flops | bytes accessed | tf_op | source)
XLA Modules:
  0.0 313.3 jit_solution(4435394938757956688)
XLA Ops:
  6.5 0.0 copy-start
  6.5 0.0 all-gather.3.cloned.1.call-start
  6.5 0.8 fusion.8
  7.4 0.3 reduce_window_sum.11
  7.7 0.1 select_reduce_fusion
  7.9 0.1 fusion.7
  8.0 0.1 reshape.122
  8.1 0.0 copy-done
  8.1 1.7 gather_fusion
  9.8 0.3 select_select_fusion
  10.1 1.0 broadcast_in_dim.76
  11.1 0.0 copy-start.1
  11.1 152.1 %all_to_all.10 = bf16[16,40,6144]{2,1,0:T(8,128)(2,1)S(1)} all-to-all(bf16[16,40,6144]{2,1,0:T(8,128)(2,1)S(1)} %bitcast.38), channel_id=1, replica_groups=mesh['expert'=16,'tensor'=32] {'expert'}, dimensions={0} | all-to-all | bytes 15728640 | tf_op jit(solution)/shard_map/all_to_all | solution.py:45
  163.3 0.0 copy-done.1
  163.3 0.0 copy-start.4
  163.3 2.5 fusion.3
  165.7 0.0 copy-done.4
  165.7 3.1 %fusion.1 = bf16[1,84,640]{2,1,0:T(8,128)(2,1)} fusion(bf16[640,6144]{1,0:T(8,128)(2,1)S(1)} %bitcast.37, bf16[1,84,6144]{2,1,0:T(8,128)(2,1)S(1)} %copy-done.4, f32[640,84]{0,1:T(8,128)S(1)} %fusion.3), kind=kOutput, calls=%fused_computation.6 | convolution fusion | flops 660925440 | bytes 9219072 | tf_op jit(solution)/shard_map/dot_general | solution.py:28
  168.9 0.0 all-gather.3.cloned.1.call-update
  168.9 0.0 copy-start.5
  168.9 101.5 %all-gather.3.cloned.1.call-done = bf16[32,84,640]{2,1,0:T(8,128)(2,1)} async-done(((bf16[1,84,640]{2,1,0:T(8,128)(2,1)}), bf16[32,84,640]{2,1,0:T(8,128)(2,1)}) %all-gather.3.cloned.1.call-update) | async-done | bytes 3440656 | tf_op jit(solution)/shard_map/all_gather | solution.py:50
  270.5 5.5 %reshape.139 = bf16[2688,640]{1,0:T(8,128)(2,1)} reshape(bf16[32,84,640]{2,1,0:T(8,128)(2,1)} %all-gather.3.cloned.1.call-done) | data formatting | bytes 6881280
  276.0 0.0 copy-done.5
  276.0 0.0 copy-start.2
  276.0 0.0 copy-start.3
  276.0 3.0 convolution_convert_fusion
  279.0 0.9 copy.18
  279.9 9.0 %all-to-all-start.1 = ((bf16[16,40,192]{2,1,0:T(8,128)(2,1)}), bf16[16,40,192]{2,1,0:T(8,128)(2,1)S(1)}, u32[]{:S(2)}, u32[]{:S(2)}) async-start(bf16[16,40,192]{2,1,0:T(8,128)(2,1)} %bitcast.9), calls=%async_computation.1 | async-start | bytes 655360 | tf_op jit(solution)/shard_map/all_to_all | solution.py:52
  288.8 0.1 fusion.9
  288.9 0.0 copy-done.2
  288.9 0.0 copy-done.3
  289.0 0.1 compare_and_fusion.1
  289.0 14.9 %all-to-all-done.1 = bf16[16,40,192]{2,1,0:T(8,128)(2,1)S(1)} async-done(((bf16[16,40,192]{2,1,0:T(8,128)(2,1)}), bf16[16,40,192]{2,1,0:T(8,128)(2,1)S(1)}, u32[]{:S(2)}, u32[]{:S(2)}) %all-to-all-start.1) | async-done | bytes 245792 | tf_op jit(solution)/shard_map/all_to_all | solution.py:52
  303.9 0.1 convert_reduce_fusion
  304.0 1.6 gather_fusion.1
  305.6 0.2 multiply_reduce_fusion
  305.8 0.7 copy.19
  (8 shorter events, 0.1 us)
Async XLA Ops:
  6.5 1.6 copy-start
  6.5 263.9 %all-gather.3.cloned.1.call-start = ((), (), s32[]{:S(2)}) async-start(), calls=%async_computation.2 | async-start | bytes 3717120 | tf_op jit(solution)/shard_map/all_gather | solution.py:50
  11.1 152.1 %copy-start.1 = (bf16[1,84,6144]{2,1,0:T(8,128)(2,1)S(1)}, bf16[1,84,6144]{2,1,0:T(8,128)(2,1)}, u32[]{:S(2)}) copy-start(bf16[1,84,6144]{2,1,0:T(8,128)(2,1)} %param.9) | copy-start | bytes 3096580
  163.3 2.5 copy-start.4
  168.9 107.1 %copy-start.5 = (bf16[1,192,2688]{2,1,0:T(8,128)(2,1)S(1)}, bf16[1,192,2688]{2,1,0:T(8,128)(2,1)}, u32[]{:S(2)}) copy-start(bf16[1,192,2688]{2,1,0:T(8,128)(2,1)} %param.11) | copy-start | bytes 3096580
  276.0 13.0 %copy-start.2 = (s32[128,4]{0,1:T(4,128)S(1)}, s32[128,4]{0,1:T(4,128)}, u32[]{:S(2)}) copy-start(s32[128,4]{0,1:T(4,128)} %param.7) | copy-start | bytes 6148
  276.0 13.0 %copy-start.3 = (f32[128,4]{0,1:T(4,128)S(1)}, f32[128,4]{0,1:T(4,128)}, u32[]{:S(2)}) copy-start(f32[128,4]{0,1:T(4,128)} %param.8) | copy-start | bytes 6148
  279.9 24.1 %all-to-all-start.1 = ((bf16[16,40,192]{2,1,0:T(8,128)(2,1)}), bf16[16,40,192]{2,1,0:T(8,128)(2,1)S(1)}, u32[]{:S(2)}, u32[]{:S(2)}) async-start(bf16[16,40,192]{2,1,0:T(8,128)(2,1)} %bitcast.9), calls=%async_computation.1 | async-start | bytes 655360 | tf_op jit(solution)/shard_map/all_to_all | solution.py:52
Sparse Core Ops, SparseCore 0:
  169.0 101.3 all-gather.2
where the time goes:
time: 314 us; the launch traced here: 313 us
  blocking collectives  152 us (48%)
  waiting for transfers between devices  116 us (37%)
  between operations  13.5 us (4%)
  local copies, waits for them, and re-layouts  11.5 us (4%)
  starting transfers between devices  8.99 us (3%)
  matrix products  8.59 us (3%)
    all_to_all x1, blocking collectives, body(): lax.all_to_all(outgoing, 'expert', split_axis=0, concat_axis=0, tiled=True)  152 us
    all_gather x1, waiting for transfers between devices, body(): lax.all_gather(hidden, 'tensor', axis=1, tiled=True)  102 us
    all_to_all x1, waiting for transfers between devices, body(): lax.all_to_all(partial_value, 'expert', split_axis=0, concat_axis=0, tile...  14.9 us
    all_to_all x1, starting transfers between devices, body(): lax.all_to_all(partial_value, 'expert', split_axis=0, concat_axis=0, tile...  8.98 us
    dot_general x3, matrix products, contract_last(): lax.dot_general(left, right, (((1,), (1,)), ((), ())), preferred_element_...  8.59 us
  transfers between devices with their start and end apart: 2, of which 2 were waited for; matrix products, arithmetic and copies ran while one was open for 0% of the time, Pallas kernels for 0%

commit v1 on v0

v1 whole, which is shorter than its diff:
```python
import jax
import jax.numpy as jnp
from jax import lax
from jax.sharding import Mesh, PartitionSpec as P

WIN = 4
CAP = 40
EXPERT = ("x", "yh")
TENSOR = ("zh", "zl", "yl", "c")
GROUP = ("zl", "yl", "c")
SIZES = (4, 4, 4, 2, 2, 2)


def slot_tables(route_block, gate_block):
    experts = jnp.arange(WIN, dtype=jnp.int32)
    hits = route_block[None, :, :] == experts[:, None, None]
    chosen = jnp.any(hits, axis=2)
    position = jnp.cumsum(chosen.astype(jnp.int32), axis=1) - 1
    slots = jnp.arange(CAP, dtype=jnp.int32)
    match = chosen[:, None, :] & (position[:, None, :] == slots[None, :, None])
    weight = jnp.sum(
        jnp.where(hits, gate_block[None, :, :], jnp.zeros((), gate_block.dtype)), axis=2
    )
    return match, weight


def contract_last(left, right):
    return lax.dot_general(
        left, right, (((1,), (1,)), ((), ())), preferred_element_type=jnp.float32
    )


def return_pairs():
    pairs = []
    for x in range(4):
        for yh in range(4):
            for q in range(8):
                turn = x * 4 + yh
                to_yh = q >> 1
                to_x = (q & 1) * 2 + (turn >> 3)
                to_q = turn & 7
                pairs.append(((x * 4 + yh) * 8 + q, (to_x * 4 + to_yh) * 8 + to_q))
    return pairs


def body(tokens, routes, gates, gate_proj, up_proj, down_proj):
    width = tokens.shape[1]
    part = width // 8
    hid = gate_proj.shape[1]
    out_w = down_proj.shape[1]
    q = lax.axis_index(GROUP)

    both = jnp.concatenate([gate_proj, up_proj], axis=0)
    both = both.reshape(2 * hid, 8, part).transpose(1, 0, 2)
    both = lax.all_to_all(both, GROUP, split_axis=0, concat_axis=0, tiled=True)
    w_gate = both[:, :hid].reshape(8 * hid, part)
    w_up = both[:, hid:].reshape(8 * hid, part)
    w_down = lax.all_gather(down_proj[0], GROUP, axis=0, tiled=True)

    match, weight = slot_tables(routes, gates)
    pick = match.reshape(WIN * CAP, -1)
    mine = lax.dynamic_slice_in_dim(tokens, q * part, part, axis=1)
    picked = jnp.dot(
        pick.astype(jnp.bfloat16), mine, preferred_element_type=jnp.float32
    ).astype(jnp.bfloat16)
    outgoing = jnp.broadcast_to(
        picked.reshape(1, WIN, CAP, part), (4, WIN, CAP, part)
    ).reshape(16, CAP, part)
    arrived = lax.all_to_all(outgoing, ("yh", "x"), split_axis=0, concat_axis=0, tiled=True)
    rows = arrived.reshape(16 * CAP, part)

    gate_part = contract_last(rows, w_gate).astype(jnp.bfloat16)
    up_part = contract_last(rows, w_up).astype(jnp.bfloat16)
    parts = jnp.concatenate([gate_part, up_part], axis=1).reshape(8, 2 * CAP, 16 * hid)
    parts = lax.all_to_all(parts, GROUP, split_axis=0, concat_axis=0, tiled=True)
    acts = jnp.sum(parts.astype(jnp.float32), axis=0)
    hidden = (jax.nn.silu(acts[:, : 8 * hid]) * acts[:, 8 * hid :]).astype(jnp.bfloat16)

    spread = jnp.broadcast_to(hidden[None], (4,) + hidden.shape)
    spread = lax.all_to_all(spread, "zh", split_axis=0, concat_axis=0, tiled=True)
    full = spread.transpose(1, 0, 2).reshape(2 * CAP, 32 * hid)
    partial_value = contract_last(full, w_down).astype(jnp.bfloat16)

    back = partial_value.reshape(2, CAP, 8, out_w).transpose(0, 2, 1, 3)
    back = back.reshape(16, CAP, out_w)
    back = lax.all_to_all(back, EXPERT, split_axis=0, concat_axis=0, tiled=True)
    summed = back.astype(jnp.float32).reshape(WIN, 4, CAP, out_w).sum(axis=1)
    summed = lax.ppermute(summed.reshape(WIN * CAP, out_w), EXPERT + GROUP, return_pairs())

    mix = jnp.where(match, weight[:, None, :], 0.0).reshape(WIN * CAP, -1)
    combined = lax.dot_general(
        mix,
        summed,
        (((0,), (0,)), ((), ())),
        precision=lax.Precision.HIGHEST,
        preferred_element_type=jnp.float32,
    )
    return combined.astype(jnp.bfloat16)


def solution(mesh):
    fine = Mesh(mesh.devices.reshape(SIZES), EXPERT + TENSOR)
    in_specs = (
        P(EXPERT, None),
        P(EXPERT, None),
        P(EXPERT, None),
        P(EXPERT, TENSOR, None),
        P(EXPERT, TENSOR, None),
        P(EXPERT, TENSOR, None),
    )
    return jax.shard_map(
        body, mesh=fine, in_specs=in_specs, out_specs=P(EXPERT, TENSOR), check_vma=False
    )
```

time: 314 us -> 217 us (0.69)
  the two profiles are of different devices: /device:TPU:8 before, /device:TPU:136 now
where the time goes in v1:
time: 217 us
  waiting for transfers between devices  81.4 us (38%)
  blocking collectives  70.2 us (32%)
  local copies, waits for them, and re-layouts  17.4 us (8%)
  starting transfers between devices  16.5 us (8%)
  between operations  13.6 us (6%)
  matrix products  12.2 us (6%)
  other arithmetic  5.47 us (3%)
    all_to_all x1, waiting for transfers between devices, body(): both = lax.all_to_all(both, GROUP, split_axis=0, concat_axis=0, tiled=True)  38.4 us
    all_to_all x1, blocking collectives, body(): lax.all_to_all(parts, GROUP, split_axis=0, concat_axis=0, tiled=True)  27.1 us
    all_to_all x1, waiting for transfers between devices, body(): lax.all_to_all(outgoing, ('yh', 'x'), split_axis=0, concat_axis=0, tiled=...  26.1 us
    all_to_all x1, blocking collectives, body(): lax.all_to_all(spread, 'zh', split_axis=0, concat_axis=0, tiled=True)  22.9 us
    all_to_all x1, blocking collectives, body(): back = lax.all_to_all(back, EXPERT, split_axis=0, concat_axis=0, tiled=True)  20.2 us
    ppermute x1, waiting for transfers between devices, body(): lax.ppermute(summed.reshape(WIN * CAP, out_w), EXPERT + GROUP, return_pai...  16.2 us
    dot_general x3, matrix products, contract_last(): lax.dot_general(left, right, (((1,), (1,)), ((), ())), preferred_element_...  10.7 us
    all_to_all x1, starting transfers between devices, body(): lax.all_to_all(outgoing, ('yh', 'x'), split_axis=0, concat_axis=0, tiled=...  9.32 us
  transfers between devices with their start and end apart: 4, of which 3 were waited for; matrix products, arithmetic and copies ran while one was open for 13% of the time, Pallas kernels for 0%

profile of v1, /device:TPU:136, one launch (start us, length us, event | category | flops | bytes accessed | tf_op | source)
XLA Modules:
  0.0 216.7 jit_solution(17203386987502061829)
XLA Ops:
  6.5 0.0 copy-start
  6.5 0.0 all-gather.3.cloned.1.call-start
  6.5 0.7 all-gather.3.cloned.1.call-update
  7.3 3.1 %pad_maximum_fusion = bf16[2,84,6144]{2,1,0:T(8,128)(2,1)} fusion(bf16[1,84,6144]{2,1,0:T(8,128)(2,1)} %param.10, bf16[1,84,6144]{2,1,0:T(8,128)(2,1)} %param.9), kind=kLoop, calls=%fused_computation.4 | loop fusion | flops 1032192 | bytes 4128768 | tf_op jit(solution)/shard_map/concatenate | solution.py:53
  10.3 3.2 %reshape.63 = bf16[168,8,768]{2,1,0:T(8,128)(2,1)} reshape(bf16[2,84,6144]{2,1,0:T(8,128)(2,1)} %pad_maximum_fusion) | data formatting | bytes 4128768 | tf_op jit(solution)/shard_map/reshape | solution.py:54
  13.6 3.3 %copy.25 = bf16[168,8,768]{2,0,1:T(8,128)(2,1)} copy(bf16[168,8,768]{2,1,0:T(8,128)(2,1)} %reshape.63) | data formatting | bytes 4128768 | tf_op jit(solution)/shard_map/reshape | solution.py:54
  16.9 0.0 copy-start.2
  16.9 5.2 %all-to-all-start.1 = ((bf16[8,168,768]{2,1,0:T(8,128)(2,1)}), bf16[8,168,768]{2,1,0:T(8,128)(2,1)}, u32[]{:S(2)}, u32[]{:S(2)}) async-start(bf16[8,168,768]{2,1,0:T(8,128)(2,1)} %bitcast.40), calls=%async_computation.1 | async-start | bytes 4128768 | tf_op jit(solution)/shard_map/all_to_all | solution.py:55
  22.1 0.0 copy-done.2
  22.2 0.3 reduce_window_sum.11
  22.5 0.1 eq.40
  22.6 0.1 fusion.7
  22.7 0.0 copy-done
  22.7 0.2 convolution_convert_fusion.2
  22.9 38.4 %all-to-all-done.1 = bf16[8,168,768]{2,1,0:T(8,128)(2,1)} async-done(((bf16[8,168,768]{2,1,0:T(8,128)(2,1)}), bf16[8,168,768]{2,1,0:T(8,128)(2,1)}, u32[]{:S(2)}, u32[]{:S(2)}) %all-to-all-start.1) | async-done | bytes 2064416 | tf_op jit(solution)/shard_map/all_to_all | solution.py:55
  61.3 1.0 broadcast_in_dim.52
  62.3 9.3 %all-to-all-start = ((bf16[16,40,768]{2,1,0:T(8,128)(2,1)}), bf16[16,40,768]{2,1,0:T(8,128)(2,1)}, u32[]{:S(2)}, u32[]{:S(2)}) async-start(bf16[16,40,768]{2,1,0:T(8,128)(2,1)} %bitcast.4), calls=%async_computation | async-start | bytes 1966080 | tf_op jit(solution)/shard_map/all_to_all | solution.py:69
  71.6 2.9 %fusion.10 = (bf16[8,84,768]{2,1,0:T(8,128)(2,1)S(1)}, bf16[8,84,768]{2,1,0:T(8,128)(2,1)}) fusion(bf16[8,168,768]{2,1,0:T(8,128)(2,1)} %all-to-all-done.1), kind=kLoop, calls=%fused_computation.23 | loop fusion | bytes 4128768 | tf_op jit(solution)/shard_map/slice | solution.py:56
  74.5 2.1 reshape.65
  76.6 1.1 reshape.64
  77.6 26.1 %all-to-all-done = bf16[16,40,768]{2,1,0:T(8,128)(2,1)} async-done(((bf16[16,40,768]{2,1,0:T(8,128)(2,1)}), bf16[16,40,768]{2,1,0:T(8,128)(2,1)}, u32[]{:S(2)}, u32[]{:S(2)}) %all-to-all-start) | async-done | bytes 983072 | tf_op jit(solution)/shard_map/all_to_all | solution.py:69
  103.8 0.0 copy-start.1
  103.8 2.6 %convolution_convert_fusion = bf16[640,672]{0,1:T(8,128)(2,1)S(1)} fusion(bf16[640,768]{1,0:T(8,128)(2,1)} %bitcast.5, bf16[672,768]{1,0:T(8,128)(2,1)} %reshape.65), kind=kOutput, calls=%fused_computation.7 | convolution fusion | flops 661032960 | bytes 2875392 | tf_op jit(solution)/shard_map/dot_general | solution.py:28
  106.4 0.0 copy-done.1
  106.4 2.2 %convolution_convert_fusion.1 = bf16[640,672]{0,1:T(8,128)(2,1)S(1)} fusion(bf16[640,768]{1,0:T(8,128)(2,1)} %bitcast.5, bf16[672,768]{1,0:T(8,128)(2,1)S(1)} %copy-done.1), kind=kOutput, calls=%fused_computation.8 | convolution fusion | flops 661032960 | bytes 2875392 | tf_op jit(solution)/shard_map/dot_general | solution.py:28
  108.6 1.4 pad_maximum_fusion.1
  110.0 2.7 %copy.21 = bf16[640,1344]{1,0:T(8,128)(2,1)S(1)} copy(bf16[640,1344]{0,1:T(8,128)(2,1)} %pad_maximum_fusion.1) | data formatting | bytes 3440640 | tf_op jit(solution)/shard_map/concatenate | solution.py:74
  112.8 27.1 %all_to_all.25 = bf16[8,80,1344]{2,1,0:T(8,128)(2,1)S(1)} all-to-all(bf16[8,80,1344]{2,1,0:T(8,128)(2,1)S(1)} %bitcast.41), channel_id=1, replica_groups=mesh['x'=4,'yh'=4,'zh'=4,'zl'=2,'yl'=2,'c'=2] {'zl','yl','c'}, dimensions={0} | all-to-all | bytes 3440640 | tf_op jit(solution)/shard_map/all_to_all | solution.py:75
  139.8 0.2 convert_reduce_fusion
  140.1 0.1 fusion.5
  140.3 22.9 %all_to_all.26 = bf16[4,80,672]{2,1,0:T(8,128)(2,1)S(1)} all-to-all(bf16[4,80,672]{2,1,0:T(8,128)(2,1)S(1)} %broadcast_in_dim.53), channel_id=1, replica_groups=mesh['x'=4,'yh'=4,'zh'=4,'zl'=2,'yl'=2,'c'=2] {'zh'}, dimensions={0} | all-to-all | bytes 860160 | tf_op jit(solution)/shard_map/all_to_all | solution.py:80
  163.2 0.3 copy.22
  163.4 0.4 reshape.67
  163.8 0.0 all-gather.3.cloned.1.call-done
  163.8 5.9 %fusion.2 = bf16[80,1536]{1,0:T(8,128)(2,1)S(1)} fusion(bf16[80,2688]{1,0:T(8,128)(2,1)S(1)} %reshape.67, bf16[1,1536,2688]{2,1,0:T(8,128)(2,1)} %all-gather.3.cloned.1.call-done), kind=kOutput, calls=%fused_computation.3 | convolution fusion | flops 660725760 | bytes 8933376 | tf_op jit(solution)/shard_map/dot_general | solution.py:28
  169.8 0.0 copy-start.3
  169.8 0.3 reshape.68
  170.0 0.1 copy.23
  170.1 20.2 %all_to_all.27 = bf16[16,40,192]{2,1,0:T(8,128)(2,1)S(1)} all-to-all(bf16[16,40,192]{2,1,0:T(8,128)(2,1)S(1)} %bitcast.43), channel_id=1, replica_groups=mesh['x'=4,'yh'=4,'zh'=4,'zl'=2,'yl'=2,'c'=2] {'x','yh'}, dimensions={0} | all-to-all | bytes 491520 | tf_op jit(solution)/shard_map/all_to_all | solution.py:86
  190.3 0.1 convert_reduce_fusion.1
  190.4 1.9 collective-permute-start
  192.3 0.0 copy-done.3
  192.4 0.1 bitcast_select_fusion
  192.4 16.2 %collective-permute-done = f32[160,192]{1,0:T(8,128)S(1)} collective-permute-done((f32[160,192]{1,0:T(8,128)S(1)}, f32[160,192]{1,0:T(8,128)S(1)}, u32[]{:S(2)}, u32[]{:S(2)}) %collective-permute-start) | collective-permute-done | bytes 122912 | tf_op jit(solution)/shard_map/ppermute | solution.py:88
  208.6 1.2 convolution_convert_fusion.3
  (6 shorter events, 0.1 us)
Async XLA Ops:
  6.5 16.1 %copy-start = (bf16[128,6144]{1,0:T(8,128)(2,1)S(1)}, bf16[128,6144]{1,0:T(8,128)(2,1)}, u32[]{:S(2)}) copy-start(bf16[128,6144]{1,0:T(8,128)(2,1)} %param.6) | copy-start | bytes 4718596
  6.5 157.3 %all-gather.3.cloned.1.call-start = ((), (), s32[]{:S(2)}) async-start(), calls=%async_computation.5 | async-start | bytes 9289728 | tf_op jit(solution)/shard_map/all_gather | solution.py:58
  16.9 5.2 %copy-start.2 = (s32[128,4]{0,1:T(4,128)S(1)}, s32[128,4]{0,1:T(4,128)}, u32[]{:S(2)}) copy-start(s32[128,4]{0,1:T(4,128)} %param.7) | copy-start | bytes 6148
  16.9 44.4 %all-to-all-start.1 = ((bf16[8,168,768]{2,1,0:T(8,128)(2,1)}), bf16[8,168,768]{2,1,0:T(8,128)(2,1)}, u32[]{:S(2)}, u32[]{:S(2)}) async-start(bf16[8,168,768]{2,1,0:T(8,128)(2,1)} %bitcast.40), calls=%async_computation.1 | async-start | bytes 4128768 | tf_op jit(solution)/shard_map/all_to_all | solution.py:55
  62.3 41.5 %all-to-all-start = ((bf16[16,40,768]{2,1,0:T(8,128)(2,1)}), bf16[16,40,768]{2,1,0:T(8,128)(2,1)}, u32[]{:S(2)}, u32[]{:S(2)}) async-start(bf16[16,40,768]{2,1,0:T(8,128)(2,1)} %bitcast.4), calls=%async_computation | async-start | bytes 1966080 | tf_op jit(solution)/shard_map/all_to_all | solution.py:69
  103.8 2.6 %copy-start.1 = (bf16[672,768]{1,0:T(8,128)(2,1)S(1)}, bf16[672,768]{1,0:T(8,128)(2,1)}, u32[]{:S(2)}) copy-start(bf16[672,768]{1,0:T(8,128)(2,1)} %reshape.64) | copy-start | bytes 3096580
  169.8 22.6 %copy-start.3 = (f32[128,4]{0,1:T(4,128)S(1)}, f32[128,4]{0,1:T(4,128)}, u32[]{:S(2)}) copy-start(f32[128,4]{0,1:T(4,128)} %param.8) | copy-start | bytes 6148
  190.4 18.2 %collective-permute-start = (f32[160,192]{1,0:T(8,128)S(1)}, f32[160,192]{1,0:T(8,128)S(1)}, u32[]{:S(2)}, u32[]{:S(2)}) collective-permute-start(f32[160,192]{1,0:T(8,128)S(1)} %bitcast.45), channel_id=1, source_target_pairs={{0,0},{1,256},{2,32},{3,288},{4,64},{5,320},{6,96},{7,352},{32,1},... | collective-permute-start | bytes 368648 | tf_op jit(solution)/shard_map/ppermute | solution.py:88
Sparse Core Ops, SparseCore 0:
  9.5 85.6 all-gather.2

commit v2 on v1

v2 whole, which is shorter than its diff:
```python
import jax
import jax.numpy as jnp
from jax import lax
from jax.experimental import pallas as pl
from jax.experimental.pallas import tpu as pltpu
from jax.sharding import Mesh, PartitionSpec as P

WIN = 4
CAP = 40
EXPERT = ("x", "yh")
TENSOR = ("zh", "zl", "yl", "c")
GROUP = ("zl", "c")
SIZES = (4, 4, 4, 2, 2, 2)
VMEM = pl.BlockSpec(memory_space=pltpu.VMEM)
SMEM = pl.BlockSpec(memory_space=pltpu.SMEM)
ANY = pl.BlockSpec(memory_space=pl.ANY)


def slot_tables(route_block, gate_block):
    experts = jnp.arange(WIN, dtype=jnp.int32)
    hits = route_block[None, :, :] == experts[:, None, None]
    chosen = jnp.any(hits, axis=2)
    position = jnp.cumsum(chosen.astype(jnp.int32), axis=1) - 1
    slots = jnp.arange(CAP, dtype=jnp.int32)
    match = chosen[:, None, :] & (position[:, None, :] == slots[None, :, None])
    weight = jnp.sum(
        jnp.where(hits, gate_block[None, :, :], jnp.zeros((), gate_block.dtype)), axis=2
    )
    return match, weight


def contract_last(left, right):
    return lax.dot_general(
        left, right, (((1,), (1,)), ((), ())), preferred_element_type=jnp.float32
    )


def swap(value, mask):
    return lax.ppermute(value, GROUP, [(i, i ^ mask) for i in range(4)])


def ring_half(i):
    return i >> 1


def expert_groups():
    return [
        [(x * 4 + yh) * 2 + (g ^ ring_half(yh)) for yh in range(4) for x in range(4)]
        for g in range(2)
    ]


def depth_groups():
    return [
        [(zh * 2 + (g ^ ring_half(zh))) * 2 + yl for zh in range(4) for yl in range(2)]
        for g in range(2)
    ]


def return_pairs():
    pairs = []
    for x in range(4):
        for yh in range(4):
            for zh in range(4):
                for zl in range(2):
                    for yl in range(2):
                        for c in range(2):
                            chunk = (zl ^ ring_half(zh)) * 2 + c
                            to_zl, to_c = yh >> 1, yh & 1
                            pairs.append(
                                (
                                    ((((x * 4 + yh) * 4 + zh) * 2 + zl) * 2 + yl) * 2 + c,
                                    ((((x * 4 + chunk) * 4 + zh) * 2 + to_zl) * 2 + yl) * 2
                                    + to_c,
                                )
                            )
    return pairs


def pieces_kernel(q_ref, g0, u0, g1, u1, o0, o1):
    hid = g0.shape[1]
    for g_ref, u_ref, o_ref in ((g0, u0, o0), (g1, u1, o1)):
        o_ref[0, :hid] = g_ref[0]
        o_ref[0, hid:] = u_ref[0]


def weight_pieces(q, gate_proj, up_proj):
    hid, width = gate_proj.shape[1:]
    part = width // 4

    def source(m):
        return pl.BlockSpec((1, hid, part), lambda r, q_ref: (0, 0, q_ref[0] ^ (2 * m + r)))

    return pl.pallas_call(
        pieces_kernel,
        out_shape=[jax.ShapeDtypeStruct((2, 2 * hid, part), gate_proj.dtype)] * 2,
        grid_spec=pltpu.PrefetchScalarGridSpec(
            num_scalar_prefetch=1,
            grid=(2,),
            in_specs=[source(0), source(0), source(1), source(1)],
            out_specs=[pl.BlockSpec((1, 2 * hid, part), lambda r, q_ref: (r, 0, 0))] * 2,
        ),
        cost_estimate=pl.CostEstimate(flops=0, bytes_accessed=8 << 20, transcendentals=0),
        name="weight_pieces",
    )(q, gate_proj, up_proj, gate_proj, up_proj)


def pack_kernel(q_ref, r0, r1, c_ref, out_ref, sems):
    q = q_ref[0]
    copies = []
    for m, r_ref in enumerate((r0, r1)):
        copies.append((r_ref.at[0], out_ref.at[(2 * m) ^ q]))
        copies.append((c_ref.at[m], out_ref.at[(2 * m + 1) ^ q]))
    copies = [
        pltpu.make_async_copy(source, target, sems.at[i])
        for i, (source, target) in enumerate(copies)
    ]
    for copy in copies:
        copy.start()
    for copy in copies:
        copy.wait()


def pack_weights(q, direct, crossed):
    both, part = crossed.shape[1:]
    packed = pl.pallas_call(
        pack_kernel,
        out_shape=jax.ShapeDtypeStruct((4, both, part), crossed.dtype),
        in_specs=[SMEM] + [ANY] * 3,
        out_specs=ANY,
        scratch_shapes=[pltpu.SemaphoreType.DMA((4,))],
        compiler_params=pltpu.CompilerParams(vmem_limit_bytes=1 << 20),
        cost_estimate=pl.CostEstimate(flops=0, bytes_accessed=4 << 20, transcendentals=0),
        name="pack_weights",
    )(q, *direct, crossed)
    return packed.reshape(4 * both, part)


def first_kernel(q_ref, x_ref, packed, other_ref, own_ref):
    core = lax.rem(q_ref[0], 2)
    flip = q_ref[1]
    width = packed.shape[0]
    rows = 4 * CAP
    for side, out_ref in ((1 - core, other_ref), (core, own_ref)):
        for m in range(2):
            start = pl.multiple_of(((2 * m) ^ flip) * rows + side * rows, 16)
            value = x_ref[pl.ds(start, rows)]
            for n in range(0, width, 256):
                stop = min(n + 256, width)
                out_ref[m, :, n:stop] = contract_last(value, packed[n:stop])


def first_matmul(q, rows, packed):
    width, part = packed.shape
    shape = jax.ShapeDtypeStruct((2, 4 * CAP, width), jnp.float32)
    return pl.pallas_call(
        first_kernel,
        out_shape=[shape, shape],
        in_specs=[SMEM, VMEM, VMEM],
        out_specs=[VMEM, VMEM],
        compiler_params=pltpu.CompilerParams(vmem_limit_bytes=24 << 20),
        cost_estimate=pl.CostEstimate(
            flops=2 * 640 * 672 * 1536, bytes_accessed=7 << 20, transcendentals=0
        ),
        name="first_matmul",
    )(q, rows, packed)


def activations_kernel(own_ref, near_ref, far_ref, out_ref):
    acts = own_ref[...] + near_ref[...] + far_ref[...].astype(jnp.float32)
    hid = acts.shape[1] // 8
    for j in range(4):
        gate = acts[:, 2 * hid * j : 2 * hid * j + hid]
        up = acts[:, 2 * hid * j + hid : 2 * hid * (j + 1)]
        hidden = ((gate / (1.0 + jnp.exp(-gate))) * up).astype(jnp.bfloat16)
        for z in range(8):
            out_ref[z, :, hid * j : hid * (j + 1)] = hidden


def activations(own, near, far):
    rows, width = own.shape
    return pl.pallas_call(
        activations_kernel,
        out_shape=jax.ShapeDtypeStruct((8, rows, width // 2), jnp.bfloat16),
        in_specs=[VMEM] * 3,
        out_specs=VMEM,
        compiler_params=pltpu.CompilerParams(vmem_limit_bytes=20 << 20),
        cost_estimate=pl.CostEstimate(
            flops=1 << 20, bytes_accessed=3 << 20, transcendentals=1 << 16
        ),
        name="activations",
    )(own, near, far)


def second_kernel(q_ref, h_ref, d0, d1, d2, d3, out_ref, full):
    q = q_ref[0]
    part = h_ref.shape[2] // 2
    for zh in range(4):
        for zl in range(2):
            for yl in range(2):
                start = ((zh * 2 + zl) * 2 + yl) * part
                full[:, start : start + part] = h_ref[
                    zh * 2 + yl, :, zl * part : (zl + 1) * part
                ]
    value = full[...]
    for k, d_ref in enumerate((d0, d1, d2, d3)):
        out_ref[k ^ q] = contract_last(value, d_ref[...]).astype(jnp.bfloat16)


def second_matmul(q, spread, downs):
    rows = spread.shape[1]
    out_w, depth = downs[0].shape
    return pl.pallas_call(
        second_kernel,
        out_shape=jax.ShapeDtypeStruct((4, rows, out_w), jnp.bfloat16),
        in_specs=[SMEM] + [VMEM] * 5,
        out_specs=VMEM,
        scratch_shapes=[pltpu.VMEM((rows, depth), jnp.bfloat16)],
        compiler_params=pltpu.CompilerParams(vmem_limit_bytes=24 << 20),
        cost_estimate=pl.CostEstimate(
            flops=2 * 160 * 768 * 2688, bytes_accessed=6 << 20, transcendentals=0
        ),
        name="second_matmul",
    )(q, spread, *downs)


def body(tokens, routes, gates, gate_proj, up_proj, down_proj):
    width = tokens.shape[1]
    part = width // 4
    out_w = down_proj.shape[1]
    q = lax.axis_index(GROUP)
    q1 = q.reshape(1)
    zl = lax.axis_index("zl")
    flip = 2 * ring_half(lax.axis_index("zh"))
    down0 = down_proj[0]

    p0, p1 = weight_pieces(q1, gate_proj, up_proj)
    direct = (p0, swap(p1, 2))
    crossed = swap(jnp.stack([d[1] for d in direct]), 1)
    packed = pack_weights(q1, direct, crossed)

    match, weight = slot_tables(routes, gates)
    pick = match.reshape(WIN * CAP, -1)
    mine = lax.dynamic_slice_in_dim(tokens, q * part, part, axis=1)
    picked = jnp.dot(
        pick.astype(jnp.bfloat16), mine, preferred_element_type=jnp.float32
    ).astype(jnp.bfloat16)
    outgoing = jnp.broadcast_to(
        picked.reshape(1, WIN, CAP, part), (4, WIN, CAP, part)
    ).reshape(16, CAP, part)
    arrived = lax.all_to_all(
        outgoing,
        ("x", "yh", "yl"),
        split_axis=0,
        concat_axis=0,
        axis_index_groups=expert_groups(),
        tiled=True,
    )
    late, crossed_now = lax.optimization_barrier((down0, crossed))
    down_z = swap(late, 2)
    cross_0 = swap(late, 1)
    cross_z = swap(down_z, 1)
    arrived, down_z, cross_0, cross_z = lax.optimization_barrier(
        (arrived, down_z, cross_0, cross_z)
    )
    rows = arrived.reshape(16 * CAP, part)

    other, own = first_matmul(jnp.stack([q, flip]), rows, packed)
    near = swap(other, 1)
    mine_own = lax.dynamic_index_in_dim(own, zl, axis=0, keepdims=False)
    mine_near = lax.dynamic_index_in_dim(near, zl, axis=0, keepdims=False)
    theirs = lax.dynamic_index_in_dim(own, 1 - zl, axis=0, keepdims=False)
    theirs += lax.dynamic_index_in_dim(near, 1 - zl, axis=0, keepdims=False)
    far = swap(theirs.astype(jnp.bfloat16), 2)
    spread = activations(mine_own, mine_near, far)

    spread = lax.all_to_all(
        spread,
        ("zh", "zl", "yl"),
        split_axis=0,
        concat_axis=0,
        axis_index_groups=depth_groups(),
        tiled=True,
    )
    back = second_matmul(q1, spread, (down0, cross_0, down_z, cross_z))
    back = back.reshape(16, CAP, out_w)
    back = lax.all_to_all(back, ("yh", "x"), split_axis=0, concat_axis=0, tiled=True)
    summed = back.astype(jnp.float32).reshape(4, WIN, CAP, out_w).sum(axis=0)
    summed = summed.astype(jnp.bfloat16).reshape(WIN * CAP, out_w)
    summed = lax.ppermute(summed, EXPERT + TENSOR, return_pairs())

    mix = jnp.where(match, weight[:, None, :], 0.0).reshape(WIN * CAP, -1)
    combined = lax.dot_general(
        mix,
        summed.astype(jnp.float32),
        (((0,), (0,)), ((), ())),
        precision=lax.Precision.HIGHEST,
        preferred_element_type=jnp.float32,
    )
    return combined.astype(jnp.bfloat16)


def solution(mesh):
    fine = Mesh(mesh.devices.reshape(SIZES), EXPERT + TENSOR)
    in_specs = (
        P(EXPERT, None),
        P(EXPERT, None),
        P(EXPERT, None),
        P(EXPERT, TENSOR, None),
        P(EXPERT, TENSOR, None),
        P(EXPERT, TENSOR, None),
    )
    return jax.shard_map(
        body, mesh=fine, in_specs=in_specs, out_specs=P(EXPERT, TENSOR), check_vma=False
    )
```

time: 217 us -> 166 us (0.76)
  the two profiles are of different devices: /device:TPU:136 before, /device:TPU:72 now
where the time goes in v2:
time: 166 us
  waiting for transfers between devices  58.1 us (35%)
  blocking collectives  58 us (35%)
  starting transfers between devices  25.6 us (15%)
  Pallas kernels  12.7 us (8%)
  local copies, waits for them, and re-layouts  7.82 us (5%)
  other arithmetic  2.06 us (1%)
    ppermute x7, waiting for transfers between devices, swap(): return lax.ppermute(value, GROUP, [(i, i ^ mask) for i in range(4)])  49.4 us
    all_to_all x1, blocking collectives, body(): lax.all_to_all(spread, ('zh', 'zl', 'yl'), split_axis=0, concat_axis=0, a...  35.8 us
    all_to_all x1, blocking collectives, body(): lax.all_to_all(back, ('yh', 'x'), split_axis=0, concat_axis=0, tiled=True)  22.3 us
    ppermute x7, starting transfers between devices, swap(): return lax.ppermute(value, GROUP, [(i, i ^ mask) for i in range(4)])  14.5 us
    all_to_all x1, starting transfers between devices, body(): lax.all_to_all(outgoing, ('x', 'yh', 'yl'), split_axis=0, concat_axis=0,...  8.83 us
    ppermute x1, waiting for transfers between devices, body(): summed = lax.ppermute(summed, EXPERT + TENSOR, return_pairs())  8.75 us
    unnamed x18, local copies, waits for them, and re-layouts  5.16 us
    pallas_call x1, Pallas kernels, first_matmul(): pl.pallas_call(first_kernel, out_shape=[shape, shape], in_specs=[SMEM, VM...  4.1 us
  transfers between devices with their start and end apart: 9, of which 6 were waited for; matrix products, arithmetic and copies ran while one was open for 2% of the time, Pallas kernels for 1%

profile of v2, /device:TPU:72, one launch (start us, length us, event | category | flops | bytes accessed | tf_op | source)
XLA Modules:
  0.0 165.8 jit_solution(7211223006546547266)
XLA Ops:
  0.0 0.0 copy-start
  0.0 0.0 copy-start.6
  0.0 2.7 %weight_pieces.1 = (bf16[2,168,1536]{2,1,0:T(8,128)(2,1)}, bf16[2,168,1536]{2,1,0:T(8,128)(2,1)}) custom-call(s32[1]{0:T(128)} %bitcast.3.q_ref, bf16[1,84,6144]{2,1,0:T(8,128)(2,1)} %g1.1, bf16[1,84,6144]{2,1,0:T(8,128)(2,1)} %u1_.1, bf16[1,84,6144]{2,1,0:T(8,128)(2,1)} %g1.1, bf16[1,84,6144]{2,1,0:T(8,128)(2,1)} %u1_.1), custom_call_target="tpu_custom_call" | custom-call | bytes 8388608 | tf_op jit(solution)/shard_map/weight_pieces/pallas_call | solution.py:94
  2.7 1.9 %collective-permute-start = (bf16[2,168,1536]{2,1,0:T(8,128)(2,1)}, bf16[2,168,1536]{2,1,0:T(8,128)(2,1)}, u32[]{:S(2)}, u32[]{:S(2)}) collective-permute-start(bf16[2,168,1536]{2,1,0:T(8,128)(2,1)} %get-tuple-element.15), channel_id=1, source_target_pairs={{0,4},{1,5},{4,0},{5,1},{2,6},{3,7},{6,2},{7,3},{8,12},{9,13},{12,... | collective-permute-start | bytes 3096584 | tf_op jit(solution)/shard_map/ppermute | solution.py:39
  4.6 0.0 copy-done.6
  4.7 0.3 reduce_window_sum.11
  5.0 0.1 eq.40
  5.1 0.1 fusion.2
  5.2 0.0 copy-done
  5.2 0.3 convolution_convert_fusion
  5.5 1.5 broadcast_in_dim.46
  7.0 0.0 copy-start.1
  7.0 8.8 %all-to-all-start = ((bf16[16,40,1536]{2,1,0:T(8,128)(2,1)}), bf16[16,40,1536]{2,1,0:T(8,128)(2,1)}, u32[]{:S(2)}, u32[]{:S(2)}) async-start(bf16[16,40,1536]{2,1,0:T(8,128)(2,1)} %bitcast.33), calls=%async_computation | async-start | bytes 3932160 | tf_op jit(solution)/shard_map/all_to_all | solution.py:251
  15.8 0.0 copy-done.1
  15.8 13.6 %collective-permute-done.r1 = bf16[2,168,1536]{2,1,0:T(8,128)(2,1)} collective-permute-done((bf16[2,168,1536]{2,1,0:T(8,128)(2,1)}, bf16[2,168,1536]{2,1,0:T(8,128)(2,1)}, u32[]{:S(2)}, u32[]{:S(2)}) %collective-permute-start) | collective-permute-done | bytes 1032224 | tf_op jit(solution)/shard_map/ppermute | solution.py:39
  29.5 1.1 slice.8
  30.5 0.1 pad_maximum_fusion
  30.7 1.9 %collective-permute-start.1 = (bf16[2,168,1536]{2,1,0:T(8,128)(2,1)S(1)}, bf16[2,168,1536]{2,1,0:T(8,128)(2,1)S(1)}, u32[]{:S(2)}, u32[]{:S(2)}) collective-permute-start(bf16[2,168,1536]{2,1,0:T(8,128)(2,1)S(1)} %pad_maximum_fusion), channel_id=1, source_target_pairs={{0,1},{1,0},{4,5},{5,4},{2,3},{3,2},{6,7},{7,6},{8,9},{9,8},{12,13... | collective-permute-start | bytes 3096584 | tf_op jit(solution)/shard_map/ppermute | solution.py:39
  32.6 2.6 %collective-permute-done.1.c_ref = bf16[2,168,1536]{2,1,0:T(8,128)(2,1)S(1)} collective-permute-done((bf16[2,168,1536]{2,1,0:T(8,128)(2,1)S(1)}, bf16[2,168,1536]{2,1,0:T(8,128)(2,1)S(1)}, u32[]{:S(2)}, u32[]{:S(2)}) %collective-permute-start.1) | collective-permute-done | bytes 1032224 | tf_op jit(solution)/shard_map/ppermute | solution.py:39
  35.2 0.0 copy-start.4
  35.2 1.0 copy-done.4
  36.2 2.2 %collective-permute-start.2 = (bf16[192,2688]{1,0:T(8,128)(2,1)}, bf16[192,2688]{1,0:T(8,128)(2,1)}, u32[]{:S(2)}, u32[]{:S(2)}) collective-permute-start(bf16[192,2688]{1,0:T(8,128)(2,1)} %bitcast.7.d0), channel_id=1, source_target_pairs={{0,4},{1,5},{4,0},{5,1},{2,6},{3,7},{6,2},{7,3},{8,12},{9,13},{12,... | collective-permute-start | bytes 3096584 | tf_op jit(solution)/shard_map/ppermute | solution.py:39
  38.4 1.9 %collective-permute-start.3 = (bf16[192,2688]{1,0:T(8,128)(2,1)}, bf16[192,2688]{1,0:T(8,128)(2,1)}, u32[]{:S(2)}, u32[]{:S(2)}) collective-permute-start(bf16[192,2688]{1,0:T(8,128)(2,1)} %bitcast.7.d0), channel_id=1, source_target_pairs={{0,1},{1,0},{4,5},{5,4},{2,3},{3,2},{6,7},{7,6},{8,9},{9,8},{12,13... | collective-permute-start | bytes 3096584 | tf_op jit(solution)/shard_map/ppermute | solution.py:39
  40.3 22.9 %collective-permute-done.2.d2 = bf16[192,2688]{1,0:T(8,128)(2,1)} collective-permute-done((bf16[192,2688]{1,0:T(8,128)(2,1)}, bf16[192,2688]{1,0:T(8,128)(2,1)}, u32[]{:S(2)}, u32[]{:S(2)}) %collective-permute-start.2) | collective-permute-done | bytes 1032224 | tf_op jit(solution)/shard_map/ppermute | solution.py:39
  63.3 1.9 %collective-permute-start.4 = (bf16[192,2688]{1,0:T(8,128)(2,1)}, bf16[192,2688]{1,0:T(8,128)(2,1)}, u32[]{:S(2)}, u32[]{:S(2)}) collective-permute-start(bf16[192,2688]{1,0:T(8,128)(2,1)} %collective-permute-done.2.d2), channel_id=1, source_target_pairs={{0,1},{1,0},{4,5},{5,4},{2,3},{3,2},{6,7},{7,6},{8,9},{9,8},{12,13... | collective-permute-start | bytes 3096584 | tf_op jit(solution)/shard_map/ppermute | solution.py:39
  65.2 0.1 pad_add_fusion.q_ref
  65.3 0.0 copy-start.5
  65.3 1.2 copy-done.5
  66.5 1.8 %pack_weights.1 = bf16[4,168,1536]{2,1,0:T(8,128)(2,1)S(1)} custom-call(s32[1]{0:T(128)} %bitcast.3.q_ref, bf16[2,168,1536]{2,1,0:T(8,128)(2,1)S(1)} %copy-done.1, bf16[2,168,1536]{2,1,0:T(8,128)(2,1)} %collective-permute-done.r1, bf16[2,168,1536]{2,1,0:T(8,128)(2,1)S(1)} %copy-done.5), custom_call_target="tpu_custom_call" | custom-call | bytes 4194304 | tf_op jit(solution)/shard_map/pack_weights/pallas_call | solution.py:126
  68.2 0.0 copy-start.2
  68.3 1.3 copy-done.2
  69.6 0.0 collective-permute-done.3.d1
  69.6 0.0 all-to-all-done
  69.6 0.0 collective-permute-done.4.d3
  69.6 0.0 copy-start.3
  69.6 1.6 copy-done.3
  71.2 4.1 %first_matmul.1 = (f32[2,160,672]{2,1,0:T(8,128)S(1)}, f32[2,160,672]{2,1,0:T(8,128)S(1)}) custom-call(s32[2]{0:T(128)S(1)} %pad_add_fusion.q_ref, bf16[640,1536]{1,0:T(8,128)(2,1)} %bitcast.8.x_ref, bf16[672,1536]{1,0:T(8,128)(2,1)S(1)} %bitcast.31), custom_call_target="tpu_custom_call" | custom-call | flops 1321205760 | bytes 7340032 | tf_op jit(solution)/shard_map/first_matmul/pallas_call | solution.py:156
  75.3 2.4 %collective-permute-start.5 = (f32[2,160,672]{2,1,0:T(8,128)S(1)}, f32[2,160,672]{2,1,0:T(8,128)}, u32[]{:S(2)}, u32[]{:S(2)}) collective-permute-start(f32[2,160,672]{2,1,0:T(8,128)S(1)} %get-tuple-element.19), channel_id=1, source_target_pairs={{0,1},{1,0},{4,5},{5,4},{2,3},{3,2},{6,7},{7,6},{8,9},{9,8},{12,13... | collective-permute-start | bytes 2580488 | tf_op jit(solution)/shard_map/ppermute | solution.py:39
  77.7 2.3 %collective-permute-done.5 = f32[2,160,672]{2,1,0:T(8,128)} collective-permute-done((f32[2,160,672]{2,1,0:T(8,128)S(1)}, f32[2,160,672]{2,1,0:T(8,128)}, u32[]{:S(2)}, u32[]{:S(2)}) %collective-permute-start.5) | collective-permute-done | bytes 860192 | tf_op jit(solution)/shard_map/ppermute | solution.py:39
  80.0 1.3 fusion.1
  81.3 2.2 %collective-permute-start.6 = (bf16[160,672]{1,0:T(8,128)(2,1)S(1)}, bf16[160,672]{1,0:T(8,128)(2,1)S(1)}, u32[]{:S(2)}, u32[]{:S(2)}) collective-permute-start(bf16[160,672]{1,0:T(8,128)(2,1)S(1)} %get-tuple-element.23), channel_id=1, source_target_pairs={{0,4},{1,5},{4,0},{5,1},{2,6},{3,7},{6,2},{7,3},{8,12},{9,13},{12,... | collective-permute-start | bytes 645128 | tf_op jit(solution)/shard_map/ppermute | solution.py:39
  83.5 7.9 %collective-permute-done.6.far_ref = bf16[160,672]{1,0:T(8,128)(2,1)S(1)} collective-permute-done((bf16[160,672]{1,0:T(8,128)(2,1)S(1)}, bf16[160,672]{1,0:T(8,128)(2,1)S(1)}, u32[]{:S(2)}, u32[]{:S(2)}) %collective-permute-start.6) | collective-permute-done | bytes 215072 | tf_op jit(solution)/shard_map/ppermute | solution.py:39
  91.4 0.4 activations.1
  91.8 35.8 %all_to_all.15.h_ref = bf16[8,160,336]{2,1,0:T(8,128)(2,1)S(1)} all-to-all(bf16[8,160,336]{2,1,0:T(8,128)(2,1)S(1)} %activations.1), channel_id=1, replica_groups={{0,2,8,10,20,22,28,30},{4,6,12,14,16,18,24,26},{1,3,9,11,21,23,29,31},{..., dimensions={0} | all-to-all | bytes 1720320 | tf_op jit(solution)/shard_map/all_to_all | solution.py:277
  127.6 0.0 copy-start.7
  127.6 0.0 copy-start.8
  127.6 3.7 %second_matmul.1 = bf16[4,160,192]{2,1,0:T(8,128)(2,1)S(1)} custom-call(s32[1]{0:T(128)} %bitcast.3.q_ref, bf16[8,160,336]{2,1,0:T(8,128)(2,1)S(1)} %all_to_all.15.h_ref, bf16[192,2688]{1,0:T(8,128)(2,1)} %bitcast.7.d0, bf16[192,2688]{1,0:T(8,128)(2,1)} %collective-permute-done.3.d1, bf16[192,2688]{1,0:T(8,128)(2,1)} %collective-permute-done.2.d2, ...), custom_call_target="tpu_custom_call" | custom-call | flops 660602880 | bytes 6291456 | tf_op jit(solution)/shard_map/second_matmul/pallas_call | solution.py:213
  131.3 22.3 %all_to_all.16 = bf16[16,40,192]{2,1,0:T(8,128)(2,1)S(1)} all-to-all(bf16[16,40,192]{2,1,0:T(8,128)(2,1)S(1)} %bitcast.32), channel_id=1, replica_groups=mesh['x'=4,'yh'=4,'zh'=4,'zl'=2,'yl'=2,'c'=2] {'yh','x'}, dimensions={0} | all-to-all | bytes 491520 | tf_op jit(solution)/shard_map/all_to_all | solution.py:287
  153.6 0.1 reduce
  153.7 2.3 %collective-permute-start.7 = (bf16[160,192]{1,0:T(8,128)(2,1)S(1)}, bf16[160,192]{1,0:T(8,128)(2,1)S(1)}, u32[]{:S(2)}, u32[]{:S(2)}) collective-permute-start(bf16[160,192]{1,0:T(8,128)(2,1)S(1)} %bitcast.36), channel_id=1, source_target_pairs={{0,0},{1,32},{2,2},{3,34},{4,64},{5,96},{6,66},{7,98},{8,8},{9,40}... | collective-permute-start | bytes 184328 | tf_op jit(solution)/shard_map/ppermute | solution.py:290
  155.9 0.0 copy-done.7
  155.9 0.0 copy-done.8
  156.0 0.1 bitcast_select_fusion
  156.1 8.7 %collective-permute-done.7 = bf16[160,192]{1,0:T(8,128)(2,1)S(1)} collective-permute-done((bf16[160,192]{1,0:T(8,128)(2,1)S(1)}, bf16[160,192]{1,0:T(8,128)(2,1)S(1)}, u32[]{:S(2)}, u32[]{:S(2)}) %collective-permute-start.7) | collective-permute-done | bytes 61472 | tf_op jit(solution)/shard_map/ppermute | solution.py:290
  164.8 1.0 convolution_convert_fusion.1
  (6 shorter events, 0.1 us)
Async XLA Ops:
  0.0 5.2 %copy-start = (bf16[128,6144]{1,0:T(8,128)(2,1)S(1)}, bf16[128,6144]{1,0:T(8,128)(2,1)}, u32[]{:S(2)}) copy-start(bf16[128,6144]{1,0:T(8,128)(2,1)} %param.6) | copy-start | bytes 4718596
  0.0 4.6 %copy-start.6 = (s32[128,4]{0,1:T(4,128)S(1)}, s32[128,4]{0,1:T(4,128)}, u32[]{:S(2)}) copy-start(s32[128,4]{0,1:T(4,128)} %param.7) | copy-start | bytes 6148
  2.7 26.7 %collective-permute-start = (bf16[2,168,1536]{2,1,0:T(8,128)(2,1)}, bf16[2,168,1536]{2,1,0:T(8,128)(2,1)}, u32[]{:S(2)}, u32[]{:S(2)}) collective-permute-start(bf16[2,168,1536]{2,1,0:T(8,128)(2,1)} %get-tuple-element.15), channel_id=1, source_target_pairs={{0,4},{1,5},{4,0},{5,1},{2,6},{3,7},{6,2},{7,3},{8,12},{9,13},{12,... | collective-permute-start | bytes 3096584 | tf_op jit(solution)/shard_map/ppermute | solution.py:39
  7.0 8.8 %copy-start.1 = (bf16[2,168,1536]{2,1,0:T(8,128)(2,1)S(1)}, bf16[2,168,1536]{2,1,0:T(8,128)(2,1)}, u32[]{:S(2)}) copy-start(bf16[2,168,1536]{2,1,0:T(8,128)(2,1)} %get-tuple-element.14.r0) | copy-start | bytes 3096580
  7.0 62.6 %all-to-all-start = ((bf16[16,40,1536]{2,1,0:T(8,128)(2,1)}), bf16[16,40,1536]{2,1,0:T(8,128)(2,1)}, u32[]{:S(2)}, u32[]{:S(2)}) async-start(bf16[16,40,1536]{2,1,0:T(8,128)(2,1)} %bitcast.33), calls=%async_computation | async-start | bytes 3932160 | tf_op jit(solution)/shard_map/all_to_all | solution.py:251
  30.7 4.5 %collective-permute-start.1 = (bf16[2,168,1536]{2,1,0:T(8,128)(2,1)S(1)}, bf16[2,168,1536]{2,1,0:T(8,128)(2,1)S(1)}, u32[]{:S(2)}, u32[]{:S(2)}) collective-permute-start(bf16[2,168,1536]{2,1,0:T(8,128)(2,1)S(1)} %pad_maximum_fusion), channel_id=1, source_target_pairs={{0,1},{1,0},{4,5},{5,4},{2,3},{3,2},{6,7},{7,6},{8,9},{9,8},{12,13... | collective-permute-start | bytes 3096584 | tf_op jit(solution)/shard_map/ppermute | solution.py:39
  35.2 1.0 copy-start.4
  36.2 27.1 %collective-permute-start.2 = (bf16[192,2688]{1,0:T(8,128)(2,1)}, bf16[192,2688]{1,0:T(8,128)(2,1)}, u32[]{:S(2)}, u32[]{:S(2)}) collective-permute-start(bf16[192,2688]{1,0:T(8,128)(2,1)} %bitcast.7.d0), channel_id=1, source_target_pairs={{0,4},{1,5},{4,0},{5,1},{2,6},{3,7},{6,2},{7,3},{8,12},{9,13},{12,... | collective-permute-start | bytes 3096584 | tf_op jit(solution)/shard_map/ppermute | solution.py:39
  38.4 31.2 %collective-permute-start.3 = (bf16[192,2688]{1,0:T(8,128)(2,1)}, bf16[192,2688]{1,0:T(8,128)(2,1)}, u32[]{:S(2)}, u32[]{:S(2)}) collective-permute-start(bf16[192,2688]{1,0:T(8,128)(2,1)} %bitcast.7.d0), channel_id=1, source_target_pairs={{0,1},{1,0},{4,5},{5,4},{2,3},{3,2},{6,7},{7,6},{8,9},{9,8},{12,13... | collective-permute-start | bytes 3096584 | tf_op jit(solution)/shard_map/ppermute | solution.py:39
  63.3 6.3 %collective-permute-start.4 = (bf16[192,2688]{1,0:T(8,128)(2,1)}, bf16[192,2688]{1,0:T(8,128)(2,1)}, u32[]{:S(2)}, u32[]{:S(2)}) collective-permute-start(bf16[192,2688]{1,0:T(8,128)(2,1)} %collective-permute-done.2.d2), channel_id=1, source_target_pairs={{0,1},{1,0},{4,5},{5,4},{2,3},{3,2},{6,7},{7,6},{8,9},{9,8},{12,13... | collective-permute-start | bytes 3096584 | tf_op jit(solution)/shard_map/ppermute | solution.py:39
  65.3 1.2 copy-start.5
  68.2 1.3 copy-start.2
  69.6 1.6 copy-start.3
  75.3 4.7 %collective-permute-start.5 = (f32[2,160,672]{2,1,0:T(8,128)S(1)}, f32[2,160,672]{2,1,0:T(8,128)}, u32[]{:S(2)}, u32[]{:S(2)}) collective-permute-start(f32[2,160,672]{2,1,0:T(8,128)S(1)} %get-tuple-element.19), channel_id=1, source_target_pairs={{0,1},{1,0},{4,5},{5,4},{2,3},{3,2},{6,7},{7,6},{8,9},{9,8},{12,13... | collective-permute-start | bytes 2580488 | tf_op jit(solution)/shard_map/ppermute | solution.py:39
  81.3 10.1 %collective-permute-start.6 = (bf16[160,672]{1,0:T(8,128)(2,1)S(1)}, bf16[160,672]{1,0:T(8,128)(2,1)S(1)}, u32[]{:S(2)}, u32[]{:S(2)}) collective-permute-start(bf16[160,672]{1,0:T(8,128)(2,1)S(1)} %get-tuple-element.23), channel_id=1, source_target_pairs={{0,4},{1,5},{4,0},{5,1},{2,6},{3,7},{6,2},{7,3},{8,12},{9,13},{12,... | collective-permute-start | bytes 645128 | tf_op jit(solution)/shard_map/ppermute | solution.py:39
  127.6 28.3 %copy-start.7 = (s32[128,4]{0,1:T(4,128)S(1)}, s32[128,4]{0,1:T(4,128)}, u32[]{:S(2)}) copy-start(s32[128,4]{0,1:T(4,128)} %param.7) | copy-start | bytes 6148
  127.6 28.4 %copy-start.8 = (f32[128,4]{0,1:T(4,128)S(1)}, f32[128,4]{0,1:T(4,128)}, u32[]{:S(2)}) copy-start(f32[128,4]{0,1:T(4,128)} %param.8) | copy-start | bytes 6148
  153.7 11.2 %collective-permute-start.7 = (bf16[160,192]{1,0:T(8,128)(2,1)S(1)}, bf16[160,192]{1,0:T(8,128)(2,1)S(1)}, u32[]{:S(2)}, u32[]{:S(2)}) collective-permute-start(bf16[160,192]{1,0:T(8,128)(2,1)S(1)} %bitcast.36), channel_id=1, source_target_pairs={{0,0},{1,32},{2,2},{3,34},{4,64},{5,96},{6,66},{7,98},{8,8},{9,40}... | collective-permute-start | bytes 184328 | tf_op jit(solution)/shard_map/ppermute | solution.py:290
